TPU v7x, 32 devices: a whole 2x2x4 slice. The times are simulated.
32 devices in a mesh: slide: 2 (over y), tile: 16 (over z, x, core).
Axes of the slice: x: 2, y: 2, z: 4, core: 2. Of those that a mesh axis runs over, the one named last changes fastest.
Arguments:
- fine_level: bfloat16 [2, 128, 256, 256], P('slide', 'tile'), may hold values from -6 to 6
- coarse_level: bfloat16 [2, 64, 128, 256], P('slide', 'tile'), may hold values from -6 to 6
- fine_kernel: bfloat16 [256, 9, 128], replicated, may hold values from -0.125 to 0.125
- coarse_kernel: bfloat16 [256, 9, 128], replicated, may hold values from -0.125 to 0.125
- fine_gain: float32 [128], replicated, may hold values from 0.25 to 1.75
- fine_offset: float32 [128], replicated, may hold values from -3 to 3
- coarse_gain: float32 [128], replicated, may hold values from 0.25 to 1.75
- coarse_offset: float32 [128], replicated, may hold values from -3 to 3
- class_kernel: bfloat16 [8, 128], replicated
- class_offset: float32 [8], replicated, may hold values from -4 to 4
- tissue_labels: int32 [2, 128, 256], P('slide', 'tile'), may hold values from -1 to 7, as said below
Outputs:
- loss: float32 [], replicated
- head_grads: float32 [12, 128], replicated
- conv_grads: float32 [256, 2, 9, 128], P('tile')
Inputs may be any that keep to these rules, and one draw needn't show every extreme that they name: `tissue_labels`: -1 marks a pixel without tissue, other values are classes.
All inputs are finite; a program needn't handle non-finite values.
Results may differ from a plain program's by a relative error of at most 0.0033.
Values may be sent and summed in bfloat16 or wider, within the bound.
A program may use at most 128 MiB of HBM per device.

v0:
```python
import jax
import jax.numpy as jnp
from jax import lax
from jax.sharding import PartitionSpec as P

GROUPS = 32
epsilon = 1e-05


def padded_2(cells, sides, width):
    for axis, dim in sides:
        count = lax.axis_size(axis)
        ends = count - 1
        head = lax.slice_in_dim(cells, 0, width, axis=dim)
        tail = lax.slice_in_dim(cells, cells.shape[dim] - width, cells.shape[dim], axis=dim)
        cells = jnp.concatenate(
            [
                lax.ppermute(tail, axis, [(i, (i + 1) % count) for i in range(ends)]),
                cells,
                lax.ppermute(head, axis, [((i + 1) % count, i) for i in range(ends)]),
            ],
            axis=dim,
        )
    return cells


def shifted(padded, height, width, position):
    row_step = position // 3
    col_step = position % 3
    return padded[row_step : row_step + height, col_step : col_step + width].reshape(
        height * width, -1
    )


def convolve(padded, kernel, height, width):
    total = jnp.zeros((height * width, kernel.shape[2]), jnp.float32)
    for position in range(9):
        total = total + jnp.dot(
            shifted(padded, height, width, position),
            kernel[:, position, :],
            preferred_element_type=jnp.float32,
        )
    return total


def group_sums(values, groups):
    return values.reshape(values.shape[0], groups, -1).sum(axis=(0, 2))


def spread(per_group, channels):
    return jnp.repeat(per_group, channels // per_group.shape[0])


def per_device(
    fine_level,
    coarse_level,
    fine_kernel,
    coarse_kernel,
    fine_gain,
    fine_offset,
    coarse_gain,
    coarse_offset,
    class_kernel,
    class_offset,
    tissue_labels,
):
    tiles = lax.axis_size("tile")
    channels = fine_kernel.shape[2]
    in_channels = fine_kernel.shape[0]
    height, width = (fine_level.shape[1], fine_level.shape[2])
    labels = tissue_labels[0].reshape(-1)
    tissue = (labels >= 0).astype(jnp.float32)
    total = lax.psum(jnp.sum(tissue), ("slide", "tile"))
    fine_rows = padded_2(fine_level[0], (("tile", 0),), 1)
    coarse_rows = padded_2(coarse_level[0], (("tile", 0),), 1)
    fine_pad = jnp.pad(fine_rows, ((0, 0), (1, 1), (0, 0)))
    coarse_pad = jnp.pad(coarse_rows, ((0, 0), (1, 1), (0, 0)))
    fine_conv = convolve(fine_pad, fine_kernel, height, width)
    coarse_conv = convolve(coarse_pad, coarse_kernel, height // 2, width // 2)
    stats = lax.psum(
        (
            group_sums(fine_conv, GROUPS),
            group_sums(fine_conv * fine_conv, GROUPS),
            group_sums(coarse_conv, GROUPS),
            group_sums(coarse_conv * coarse_conv, GROUPS),
        ),
        "tile",
    )
    fine_number = height * tiles * width * (channels // GROUPS)
    coarse_number = fine_number // 4

    def normalize(conv_out, first_sum, square_sum, number, gain, offset):
        mean = first_sum / number
        variance = square_sum / number - mean * mean
        scale = spread(lax.rsqrt(variance + epsilon), channels)
        normed = (conv_out - spread(mean, channels)) * scale
        return (normed, scale, normed * gain + offset)

    fine_normed, fine_scale, fine_pre = normalize(
        fine_conv, stats[0], stats[1], fine_number, fine_gain, fine_offset
    )
    coarse_normed, coarse_scale, coarse_pre = normalize(
        coarse_conv, stats[2], stats[3], coarse_number, coarse_gain, coarse_offset
    )
    act_coarse = jnp.maximum(coarse_pre, 0.0).reshape(height // 2, width // 2, channels)
    upsampled = jnp.repeat(jnp.repeat(act_coarse, 2, 0), 2, 1).reshape(height * width, channels)
    merged = (jnp.maximum(fine_pre, 0.0) + upsampled).astype(jnp.bfloat16)
    logits = (
        lax.dot_general(
            class_kernel, merged, (((1,), (1,)), ((), ())), preferred_element_type=jnp.float32
        )
        + class_offset[:, None]
    )
    onehot = (
        labels[None, :] == jnp.arange(class_kernel.shape[0], dtype=jnp.int32)[:, None]
    ).astype(jnp.float32)
    top = jnp.max(logits, axis=0)
    lse = top + jnp.log(jnp.sum(jnp.exp(logits - top[None, :]), axis=0))
    loss_local = jnp.sum((lse - jnp.sum(onehot * logits, axis=0)) * tissue)
    dlogits = ((jnp.exp(logits - lse[None, :]) - onehot) * tissue[None, :] / total).astype(
        jnp.bfloat16
    )
    class_grad = jnp.dot(dlogits, merged, preferred_element_type=jnp.float32)
    dmerged = lax.dot_general(
        dlogits, class_kernel, (((0,), (0,)), ((), ())), preferred_element_type=jnp.float32
    )
    dact_coarse = (
        dmerged.reshape(height // 2, 2, width // 2, 2, channels)
        .sum(axis=(1, 3))
        .reshape(-1, channels)
    )
    fine_dpre = dmerged * (fine_pre > 0).astype(jnp.float32)
    coarse_dpre = dact_coarse * (coarse_pre > 0).astype(jnp.float32)
    fine_dnorm = fine_dpre * fine_gain
    coarse_dnorm = coarse_dpre * coarse_gain
    back = lax.psum(
        (
            group_sums(fine_dnorm, GROUPS),
            group_sums(fine_dnorm * fine_normed, GROUPS),
            group_sums(coarse_dnorm, GROUPS),
            group_sums(coarse_dnorm * coarse_normed, GROUPS),
        ),
        "tile",
    )
    fine_dconv = (
        (
            fine_dnorm
            - spread(back[0] / fine_number, channels)
            - fine_normed * spread(back[1] / fine_number, channels)
        )
        * fine_scale
    ).astype(jnp.bfloat16)
    coarse_dconv = (
        (
            coarse_dnorm
            - spread(back[2] / coarse_number, channels)
            - coarse_normed * spread(back[3] / coarse_number, channels)
        )
        * coarse_scale
    ).astype(jnp.bfloat16)
    head_local = jnp.concatenate(
        [
            jnp.stack(
                [
                    jnp.sum(fine_dpre * fine_normed, axis=0),
                    jnp.sum(fine_dpre, axis=0),
                    jnp.sum(coarse_dpre * coarse_normed, axis=0),
                    jnp.sum(coarse_dpre, axis=0),
                ],
                0,
            ),
            class_grad,
        ],
        0,
    )
    head_grads, loss_total = lax.psum((head_local, loss_local), ("slide", "tile"))
    sections = []
    for padded, upstream, rows_here, cols_here in (
        (fine_pad, fine_dconv, height, width),
        (coarse_pad, coarse_dconv, height // 2, width // 2),
    ):
        stacked = jnp.concatenate(
            [shifted(padded, rows_here, cols_here, position) for position in range(9)], 1
        )
        product = lax.dot_general(
            stacked, upstream, (((0,), (0,)), ((), ())), preferred_element_type=jnp.float32
        )
        sections.append(product.reshape(9, in_channels, channels).transpose(1, 0, 2))
    whole = lax.psum(jnp.stack(sections, 1), "slide")
    conv_grads = lax.psum_scatter(whole, "tile", scatter_dimension=0, tiled=True)
    return (loss_total / total, head_grads, conv_grads)


def solution(mesh):
    return jax.shard_map(
        per_device,
        mesh=mesh,
        in_specs=(
            P("slide", "tile", None, None),
            P("slide", "tile", None, None),
            P(),
            P(),
            P(),
            P(),
            P(),
            P(),
            P(),
            P(),
            P("slide", "tile", None),
        ),
        out_specs=(P(), P(), P("tile", None, None, None)),
        check_vma=False,
    )
```

profile of v0, /device:TPU:0, one launch (start us, length us, event | category | flops | bytes accessed | tf_op | source)
XLA Modules:
  0.0 292.0 jit_solution(8008616227894665407)
XLA Ops:
  8.1 2.4 collective-permute-start.2
  10.5 1.3 collective-permute-start.3
  12.8 5.3 %collective-permute-start = (bf16[1,256,256]{2,1,0:T(8,128)(2,1)S(1)}, bf16[1,256,256]{2,1,0:T(8,128)(2,1)S(1)}, u32[]{:S(2)}, u32[]{:S(2)}) collective-permute-start(bf16[1,256,256]{2,1,0:T(8,128)(2,1)S(1)} %get-tuple-element.43), channel_id=1, source_target_pairs={{0,1},{1,2},{2,3},{3,4},{4,5},{5,6},{6,7},{7,8},{8,9},{9,10},{10,1... | collective-permute-start | bytes 393224 | tf_op jit(solution)/shard_map/ppermute | solution.py:18
  18.1 1.3 collective-permute-start.1
  34.2 1.3 constant_dynamic-update-slice_fusion.8
  39.5 1.6 fusion.80
  41.6 34.9 %all-reduce.4 = (f32[32]{0:T(128)S(1)}, f32[32]{0:T(128)S(1)}, f32[32]{0:T(128)S(1)}, f32[32]{0:T(128)S(1)}) all-reduce(f32[32]{0:T(128)S(1)} %copy-done.30, f32[32]{0:T(128)S(1)} %copy-done.29, f32[32]{0:T(128)S(1)} %reduce_sum.178, f32[32]{0:T(128)S(1)} %reduce_sum.175), channel_id=1, replica_groups=mesh['slide'=2,'tile'=16] {'tile'}, use_global_device_ids=true, to_apply=%region_11.12 | all-reduce | flops 128 | bytes 1024 | tf_op jit(solution)/shard_map/psum | solution.py:80
  80.5 37.0 %psum.89 = f32[]{:T(128)} all-reduce(f32[]{:T(128)} %get-tuple-element.20), channel_id=1, replica_groups=mesh['slide'=2,'tile'=16] {'slide','tile'}, use_global_device_ids=true, to_apply=%region_18.19 | all-reduce | flops 1 | bytes 8 | tf_op jit(solution)/shard_map/psum | solution.py:73
  117.5 4.0 %multiply_reduce_fusion.3 = (f32[128]{0:T(128)S(1)}, f32[128]{0:T(128)}, f32[128]{0:T(128)}, f32[128]{0:T(128)S(1)}, f32[2048,128]{1,0:T(8,128)}) fusion(f32[128]{0:T(128)} %param.15, f32[128]{0:T(128)} %param.16, f32[128]{0:T(128)} %copy-done.25, f32[2048,128]{1,0:T(8,128)} %get-tuple-element.60, f32[128]{0:T(128)} %copy-done.27, ...), kind=kOutput, calls=%fused_computation.38 | convolution fusion | flops 7716352 | bytes 2193412 | tf_op jit(solution)/shard_map/dot_general | solution.py:124
  122.0 2.7 reduce_sum.227
  124.7 1.8 multiply_reduce_fusion.4
  126.9 32.5 %all-reduce.3 = (f32[32]{0:T(128)S(1)}, f32[32]{0:T(128)S(1)}, f32[32]{0:T(128)S(1)}, f32[32]{0:T(128)S(1)}) all-reduce(f32[32]{0:T(128)S(1)} %reduce_sum.241, f32[32]{0:T(128)S(1)} %reduce_sum.238, f32[32]{0:T(128)S(1)} %reduce_sum.235, f32[32]{0:T(128)S(1)} %reduce_sum.232), channel_id=1, replica_groups=mesh['slide'=2,'tile'=16] {'tile'}, use_global_device_ids=true, to_apply=%region_36.37 | all-reduce | flops 128 | bytes 1024 | tf_op jit(solution)/shard_map/psum | solution.py:136
  160.2 2.5 constant_dynamic-update-slice_fusion.7
  163.8 1.1 constant_dynamic-update-slice_fusion.5
  164.9 1.1 constant_dynamic-update-slice_fusion.4
  167.1 1.2 constant_dynamic-update-slice_fusion.2
  168.4 1.1 constant_dynamic-update-slice_fusion.1
  169.5 1.2 constant_dynamic-update-slice_fusion
  170.7 5.4 %fusion.9 = f32[2304,128]{1,0:T(8,128)S(1)} fusion(bf16[2048,2304]{1,0:T(8,128)(2,1)} %constant_dynamic-update-slice_fusion, f32[2048,128]{1,0:T(8,128)S(1)} %copy-done.15, f32[128]{0:T(128)S(1)} %mul.148, f32[128]{0:T(128)S(1)} %sub.99, f32[128]{0:T(128)S(1)} %copy-done.35, f32[128]{0:T(128)S(1)} %copy-done.26, f32[128]{0:T(128)S(1)} %copy-done.28, ...), kind=kOutput, calls=%fused_computation.40 | convolution fusion | flops 1211105280 | bytes 12717056 | tf_op jit(solution)/shard_map/dot_general | solution.py:185
  176.1 2.5 fusion.21
  178.6 1.6 pad_maximum_fusion
  180.3 59.6 %reduce-scatter.2.cloned.1.call-done = f32[16,2,9,128]{3,0,2,1:T(8,128)} async-done(((f32[256,2,9,128]{3,0,2,1:T(8,128)}), f32[16,2,9,128]{3,0,2,1:T(8,128)}) %reduce-scatter.2.cloned.1.call-update) | async-done | bytes 147472 | tf_op jit(solution)/shard_map/reduce_scatter | solution.py:190
  240.9 40.0 %all-reduce.2 = (f32[]{:T(128)}, f32[12,128]{1,0:T(8,128)}) all-reduce(f32[]{:T(128)} %get-tuple-element.21, f32[12,128]{1,0:T(8,128)S(1)} %concatenate.33), channel_id=1, replica_groups=mesh['slide'=2,'tile'=16] {'slide','tile'}, use_global_device_ids=true, to_apply=%region_16.17 | all-reduce | flops 1537 | bytes 12296 | tf_op jit(solution)/shard_map/psum | solution.py:176
  282.3 1.6 copy.16
  (173 shorter events, 29.6 us)
Async XLA Ops:
  7.2 72.4 %copy-start = (bf16[8,128]{1,0:T(8,128)(2,1)S(1)}, bf16[8,128]{1,0:T(8,128)(2,1)}, u32[]{:S(2)}) copy-start(bf16[8,128]{1,0:T(8,128)(2,1)} %param.19) | copy-start | bytes 6148
  7.2 232.8 %reduce-scatter.2.cloned.1.call-start = ((), (), s32[]{:S(2)}) async-start(), calls=%async_computation.1 | async-start | bytes 2506752 | tf_op jit(solution)/shard_map/reduce_scatter | solution.py:190
  8.1 12.6 %collective-permute-start.2 = (bf16[1,128,256]{2,1,0:T(8,128)(2,1)S(1)}, bf16[1,128,256]{2,1,0:T(8,128)(2,1)S(1)}, u32[]{:S(2)}, u32[]{:S(2)}) collective-permute-start(bf16[1,128,256]{2,1,0:T(8,128)(2,1)S(1)} %get-tuple-element.53), channel_id=1, source_target_pairs={{0,1},{1,2},{2,3},{3,4},{4,5},{5,6},{6,7},{7,8},{8,9},{9,10},{10,1... | collective-permute-start | bytes 196616 | tf_op jit(solution)/shard_map/ppermute | solution.py:18
  10.5 10.2 %collective-permute-start.3 = (bf16[1,128,256]{2,1,0:T(8,128)(2,1)S(1)}, bf16[1,128,256]{2,1,0:T(8,128)(2,1)S(1)}, u32[]{:S(2)}, u32[]{:S(2)}) collective-permute-start(bf16[1,128,256]{2,1,0:T(8,128)(2,1)S(1)} %get-tuple-element.54), channel_id=1, source_target_pairs={{1,0},{2,1},{3,2},{4,3},{5,4},{6,5},{7,6},{8,7},{9,8},{10,9},{11,1... | collective-permute-start | bytes 196616 | tf_op jit(solution)/shard_map/ppermute | solution.py:20
  12.8 9.9 %copy-start.19 = (bf16[256,9,128]{2,0,1:T(8,128)(2,1)S(1)}, bf16[256,9,128]{2,0,1:T(8,128)(2,1)}, u32[]{:S(2)}) copy-start(bf16[256,9,128]{2,0,1:T(8,128)(2,1)} %param.14) | copy-start | bytes 1769476
  12.8 19.7 %collective-permute-start = (bf16[1,256,256]{2,1,0:T(8,128)(2,1)S(1)}, bf16[1,256,256]{2,1,0:T(8,128)(2,1)S(1)}, u32[]{:S(2)}, u32[]{:S(2)}) collective-permute-start(bf16[1,256,256]{2,1,0:T(8,128)(2,1)S(1)} %get-tuple-element.43), channel_id=1, source_target_pairs={{0,1},{1,2},{2,3},{3,4},{4,5},{5,6},{6,7},{7,8},{8,9},{9,10},{10,1... | collective-permute-start | bytes 393224 | tf_op jit(solution)/shard_map/ppermute | solution.py:18
  18.1 14.4 %collective-permute-start.1 = (bf16[1,256,256]{2,1,0:T(8,128)(2,1)S(1)}, bf16[1,256,256]{2,1,0:T(8,128)(2,1)S(1)}, u32[]{:S(2)}, u32[]{:S(2)}) collective-permute-start(bf16[1,256,256]{2,1,0:T(8,128)(2,1)S(1)} %get-tuple-element.44), channel_id=1, source_target_pairs={{1,0},{2,1},{3,2},{4,3},{5,4},{6,5},{7,6},{8,7},{9,8},{10,9},{11,1... | collective-permute-start | bytes 393224 | tf_op jit(solution)/shard_map/ppermute | solution.py:20
  27.2 5.9 %copy-start.1 = (bf16[1,8,256,256]{3,2,1,0:T(8,128)(2,1)S(1)}, bf16[1,8,256,256]{3,2,1,0:T(8,128)(2,1)}, u32[]{:S(2)}) copy-start(bf16[1,8,256,256]{3,2,1,0:T(8,128)(2,1)} %param.11) | copy-start | bytes 3145732
  34.2 2.9 %copy-start.4 = (bf16[8,256,256]{2,1,0:T(8,128)(2,1)}, bf16[8,256,256]{2,1,0:T(8,128)(2,1)S(1)}, u32[]{:S(2)}) copy-start(bf16[8,256,256]{2,1,0:T(8,128)(2,1)S(1)} %get-tuple-element.38) | copy-start | bytes 3145732
  34.2 3.5 %copy-start.2 = (bf16[8,256,256]{2,1,0:T(8,128)(2,1)}, bf16[8,256,256]{2,1,0:T(8,128)(2,1)S(1)}, u32[]{:S(2)}) copy-start(bf16[8,256,256]{2,1,0:T(8,128)(2,1)S(1)} %get-tuple-element.37) | copy-start | bytes 3145732
  36.7 2.8 copy-start.8
  39.5 37.7 %copy-start.24 = (f32[128]{0:T(128)S(1)}, f32[128]{0:T(128)}, u32[]{:S(2)}) copy-start(f32[128]{0:T(128)} %param.17) | copy-start | bytes 1540
  39.5 37.7 %copy-start.31 = (f32[128]{0:T(128)S(1)}, f32[128]{0:T(128)}, u32[]{:S(2)}) copy-start(f32[128]{0:T(128)} %param.18) | copy-start | bytes 1540
  41.1 36.7 %copy-start.32 = (f32[128]{0:T(128)S(1)}, f32[128]{0:T(128)}, u32[]{:S(2)}) copy-start(f32[128]{0:T(128)} %param.16) | copy-start | bytes 1540
  41.1 36.7 %copy-start.34 = (f32[128]{0:T(128)S(1)}, f32[128]{0:T(128)}, u32[]{:S(2)}) copy-start(f32[128]{0:T(128)} %param.15) | copy-start | bytes 1540
  77.4 2.5 copy-start.23
  77.4 40.1 %copy-start.22 = (f32[2048]{0:T(1024)S(1)}, f32[2048]{0:T(1024)}, u32[]{:S(2)}) copy-start(f32[2048]{0:T(1024)} %compare_convert_fusion) | copy-start | bytes 24580
  160.2 2.5 copy-start.5
  160.2 3.6 %copy-start.3 = (bf16[8,256,256]{2,1,0:T(8,128)(2,1)S(1)}, bf16[8,256,256]{2,1,0:T(8,128)(2,1)}, u32[]{:S(2)}) copy-start(bf16[8,256,256]{2,1,0:T(8,128)(2,1)} %copy-done.2) | copy-start | bytes 3145732
  170.7 5.4 %copy-start.16 = (f32[512,128]{1,0:T(8,128)S(1)}, f32[512,128]{1,0:T(8,128)}, u32[]{:S(2)}) copy-start(f32[512,128]{1,0:T(8,128)} %get-tuple-element.32) | copy-start | bytes 786436
  180.2 59.7 %copy-start.13 = (bf16[2048,128]{1,0:T(8,128)(2,1)S(1)}, bf16[2048,128]{1,0:T(8,128)(2,1)}, u32[]{:S(2)}) copy-start(bf16[2048,128]{1,0:T(8,128)(2,1)} %copy-done.12) | copy-start | bytes 1572868
  180.3 60.6 %copy-start.36 = (f32[128]{0:T(128)S(1)}, f32[128]{0:T(128)}, u32[]{:S(2)}) copy-start(f32[128]{0:T(128)} %get-tuple-element.7) | copy-start | bytes 1540
  180.3 60.6 %copy-start.37 = (f32[128]{0:T(128)S(1)}, f32[128]{0:T(128)}, u32[]{:S(2)}) copy-start(f32[128]{0:T(128)} %get-tuple-element.8) | copy-start | bytes 1540
  180.3 102.1 %all-reduce.7.cloned.1.call-start = ((), (), s32[]{:S(2)}) async-start(), calls=%async_computation.2 | async-start | bytes 294912 | tf_op jit(solution)/shard_map/psum | solution.py:189
  (21 other events, 38.6 us)
Sparse Core Ops, SparseCore 0:
  180.4 59.5 reduce-scatter.1
  242.2 20.6 all-reduce.6
where the time goes:
time: 293 us; the launch traced here: 292 us
  blocking collectives  144 us (49%)
  waiting for transfers between devices  59.7 us (20%)
  local copies, waits for them, and re-layouts  28.9 us (10%)
  matrix products  20 us (7%)
  between operations  17.3 us (6%)
  other arithmetic  11.3 us (4%)
  starting transfers between devices  10.3 us (4%)
    reduce_scatter x1, waiting for transfers between devices, per_device(): lax.psum_scatter(whole, 'tile', scatter_dimension=0, tiled=True)  59.6 us
    psum x1, blocking collectives, per_device(): lax.psum((head_local, loss_local), ('slide', 'tile'))  40 us
    psum x1, blocking collectives, per_device(): total = lax.psum(jnp.sum(tissue), ('slide', 'tile'))  37 us
    psum x1, blocking collectives, per_device(): lax.psum((group_sums(fine_conv, GROUPS), group_sums(fine_conv * fine_conv...  34.9 us
    psum x1, blocking collectives, per_device(): lax.psum((group_sums(fine_dnorm, GROUPS), group_sums(fine_dnorm * fine_no...  32.5 us
    unnamed x96, local copies, waits for them, and re-layouts  21.5 us
    dot_general x2, matrix products, per_device(): lax.dot_general(stacked, upstream, (((0,), (0,)), ((), ())), preferred_el...  7.89 us
    ppermute x2, starting transfers between devices, padded_2(): lax.ppermute(tail, axis, [(i, (i + 1) % count) for i in range(ends)])  7.66 us
  transfers between devices with their start and end apart: 6, of which 1 were waited for; matrix products, arithmetic and copies ran while one was open for 5% of the time, Pallas kernels for 0%

commit v1 on v0

--- a/solution.py
+++ b/solution.py
@@ -173,7 +173,13 @@
         ],
         0,
     )
-    head_grads, loss_total = lax.psum((head_local, loss_local), ("slide", "tile"))
+
+    def recover_positions(frame):
+        prior = jax.lax.psum(frame, axis_name="tile")
+        local_next = jax.lax.psum(prior, axis_name="slide")
+        return local_next
+
+    head_grads, loss_total = recover_positions((head_local, loss_local))
     sections = []
     for padded, upstream, rows_here, cols_here in (
         (fine_pad, fine_dconv, height, width),

time: 293 us -> 303 us (1.034)
  waiting for transfers between devices: 59.7 us -> 75.5 us
  blocking collectives: 144 us -> 138 us
    psum x1, waiting for transfers between devices: 0.02 us -> 15.9 us  [per_device(): whole = lax.psum(jnp.stack(sections, 1), 'slide')]
    psum x2, blocking collectives: 72.6 us -> 66.2 us  [the longest x1 60.4 us: recover_positions(): prior = jax.lax.psum(frame, axis_name='tile')]
  transfers between devices with their start and end apart: 6 -> 6, of which waited for: 1 -> 2; matrix products, arithmetic and copies ran while one was open for 5% -> 5% of each run, Pallas kernels for 0% -> 0%
where the time goes in v1:
time: 303 us; the launch traced here: 302 us
  blocking collectives  138 us (46%)
  waiting for transfers between devices  75.5 us (25%)
  local copies, waits for them, and re-layouts  29 us (10%)
  matrix products  20.5 us (7%)
  between operations  17.3 us (6%)
  other arithmetic  11.3 us (4%)
  starting transfers between devices  10.3 us (3%)
    psum x1, blocking collectives, recover_positions(): prior = jax.lax.psum(frame, axis_name='tile')  60.4 us
    reduce_scatter x1, waiting for transfers between devices, per_device(): lax.psum_scatter(whole, 'tile', scatter_dimension=0, tiled=True)  59.6 us
    psum x1, blocking collectives, per_device(): total = lax.psum(jnp.sum(tissue), ('slide', 'tile'))  37 us
    psum x1, blocking collectives, per_device(): lax.psum((group_sums(fine_conv, GROUPS), group_sums(fine_conv * fine_conv...  34.9 us
    unnamed x96, local copies, waits for them, and re-layouts  21.6 us
    psum x1, waiting for transfers between devices, per_device(): whole = lax.psum(jnp.stack(sections, 1), 'slide')  15.9 us
    dot_general x2, matrix products, per_device(): lax.dot_general(stacked, upstream, (((0,), (0,)), ((), ())), preferred_el...  7.89 us
    ppermute x2, starting transfers between devices, padded_2(): lax.ppermute(tail, axis, [(i, (i + 1) % count) for i in range(ends)])  7.66 us
  transfers between devices with their start and end apart: 6, of which 2 were waited for; matrix products, arithmetic and copies ran while one was open for 5% of the time, Pallas kernels for 0%

profile of v1, /device:TPU:0, one launch (start us, length us, event | category | flops | bytes accessed | tf_op | source)
XLA Modules:
  0.0 302.0 jit_solution(8447467888476895846)
XLA Ops:
  8.1 2.4 collective-permute-start.2
  10.5 1.3 collective-permute-start.3
  12.8 5.3 %collective-permute-start = (bf16[1,256,256]{2,1,0:T(8,128)(2,1)S(1)}, bf16[1,256,256]{2,1,0:T(8,128)(2,1)S(1)}, u32[]{:S(2)}, u32[]{:S(2)}) collective-permute-start(bf16[1,256,256]{2,1,0:T(8,128)(2,1)S(1)} %get-tuple-element.45), channel_id=1, source_target_pairs={{0,1},{1,2},{2,3},{3,4},{4,5},{5,6},{6,7},{7,8},{8,9},{9,10},{10,1... | collective-permute-start | bytes 393224 | tf_op jit(solution)/shard_map/ppermute | solution.py:18
  18.1 1.3 collective-permute-start.1
  38.4 1.6 fusion.80
  40.5 34.9 %all-reduce.3 = (f32[32]{0:T(128)S(1)}, f32[32]{0:T(128)S(1)}, f32[32]{0:T(128)S(1)}, f32[32]{0:T(128)S(1)}) all-reduce(f32[32]{0:T(128)S(1)} %copy-done.31, f32[32]{0:T(128)S(1)} %copy-done.30, f32[32]{0:T(128)S(1)} %reduce_sum.178, f32[32]{0:T(128)S(1)} %reduce_sum.175), channel_id=1, replica_groups=mesh['slide'=2,'tile'=16] {'tile'}, use_global_device_ids=true, to_apply=%region_11.12 | all-reduce | flops 128 | bytes 1024 | tf_op jit(solution)/shard_map/psum | solution.py:80
  79.4 37.0 %psum.104 = f32[]{:T(128)} all-reduce(f32[]{:T(128)} %get-tuple-element.20), channel_id=1, replica_groups=mesh['slide'=2,'tile'=16] {'slide','tile'}, use_global_device_ids=true, to_apply=%region_19.20 | all-reduce | flops 1 | bytes 8 | tf_op jit(solution)/shard_map/psum | solution.py:73
  116.4 2.0 fusion.75
  118.4 3.4 %multiply_reduce_fusion.3 = (f32[128]{0:T(128)S(1)}, f32[128]{0:T(128)S(1)}, f32[128]{0:T(128)S(1)}, f32[128]{0:T(128)S(1)}, f32[2048,128]{1,0:T(8,128)}) fusion(f32[128]{0:T(128)} %param.15, f32[128]{0:T(128)} %param.16, f32[128]{0:T(128)} %copy-done.26, f32[2048,128]{1,0:T(8,128)} %get-tuple-element.62, f32[128]{0:T(128)} %copy-done.28, ...), kind=kOutput, calls=%fused_computation.38 | convolution fusion | flops 7716352 | bytes 2193412 | tf_op jit(solution)/shard_map/dot_general | solution.py:124
  121.8 1.2 constant_dynamic-update-slice_fusion.8
  123.4 2.7 reduce_sum.227
  126.2 1.8 multiply_reduce_fusion.4
  128.5 60.4 %all-reduce.2 = (f32[]{:T(128)}, f32[12,128]{1,0:T(8,128)S(1)}, f32[32]{0:T(128)S(1)}, f32[32]{0:T(128)S(1)}, f32[32]{0:T(128)S(1)}, /*index=5*/f32[32]{0:T(128)S(1)}) all-reduce(f32[]{:T(128)} %get-tuple-element.21, f32[12,128]{1,0:T(8,128)S(1)} %concatenate.33, ...), channel_id=1, replica_groups=mesh['slide'=2,'tile'=16] {'tile'}, use_global_device_ids=true, to_apply=%region_16.17 | all-reduce | flops 1665 | bytes 13320 | tf_op jit(solution)/shard_map/psum | solution.py:178
  189.6 2.5 constant_dynamic-update-slice_fusion.7
  196.5 1.2 constant_dynamic-update-slice_fusion.2
  197.8 1.1 constant_dynamic-update-slice_fusion.1
  198.9 1.2 constant_dynamic-update-slice_fusion
  200.1 5.4 %fusion.9 = f32[2304,128]{1,0:T(8,128)S(1)} fusion(bf16[2048,2304]{1,0:T(8,128)(2,1)} %constant_dynamic-update-slice_fusion, f32[2048,128]{1,0:T(8,128)S(1)} %copy-done.16, f32[128]{0:T(128)S(1)} %mul.148, f32[128]{0:T(128)S(1)} %sub.99, f32[128]{0:T(128)S(1)} %copy-done.37, f32[128]{0:T(128)S(1)} %copy-done.27, f32[128]{0:T(128)S(1)} %copy-done.29, ...), kind=kOutput, calls=%fused_computation.40 | convolution fusion | flops 1211105280 | bytes 12717056 | tf_op jit(solution)/shard_map/dot_general | solution.py:191
  205.6 2.5 fusion.21
  208.0 1.6 pad_maximum_fusion
  209.8 59.6 %reduce-scatter.2.cloned.1.call-done = f32[16,2,9,128]{3,0,2,1:T(8,128)} async-done(((f32[256,2,9,128]{3,0,2,1:T(8,128)}), f32[16,2,9,128]{3,0,2,1:T(8,128)}) %reduce-scatter.2.cloned.1.call-update) | async-done | bytes 147472 | tf_op jit(solution)/shard_map/reduce_scatter | solution.py:196
  269.4 5.8 %all-reduce.4 = (f32[]{:T(128)}, f32[12,128]{1,0:T(8,128)}) all-reduce(f32[]{:T(128)} %get-tuple-element.22, f32[12,128]{1,0:T(8,128)S(1)} %get-tuple-element.23), channel_id=1, replica_groups=mesh['slide'=2,'tile'=16] {'slide'}, use_global_device_ids=true, to_apply=%region_17.18 | all-reduce | flops 1537 | bytes 12296 | tf_op jit(solution)/shard_map/psum | solution.py:179
  276.5 15.9 %all-reduce.7.cloned.1.call-done = f32[16,2,9,128]{3,0,2,1:T(8,128)} async-done(((f32[16,2,9,128]{3,0,2,1:T(8,128)}), f32[16,2,9,128]{3,0,2,1:T(8,128)}) %all-reduce.7.cloned.1.call-update) | async-done | bytes 147472 | tf_op jit(solution)/shard_map/psum | solution.py:195
  292.4 1.6 copy.16
  (173 shorter events, 31.2 us)
Async XLA Ops:
  7.2 71.3 %copy-start = (bf16[8,128]{1,0:T(8,128)(2,1)S(1)}, bf16[8,128]{1,0:T(8,128)(2,1)}, u32[]{:S(2)}) copy-start(bf16[8,128]{1,0:T(8,128)(2,1)} %param.19) | copy-start | bytes 6148
  7.2 262.2 %reduce-scatter.2.cloned.1.call-start = ((), (), s32[]{:S(2)}) async-start(), calls=%async_computation.1 | async-start | bytes 2506752 | tf_op jit(solution)/shard_map/reduce_scatter | solution.py:196
  8.1 12.6 %collective-permute-start.2 = (bf16[1,128,256]{2,1,0:T(8,128)(2,1)S(1)}, bf16[1,128,256]{2,1,0:T(8,128)(2,1)S(1)}, u32[]{:S(2)}, u32[]{:S(2)}) collective-permute-start(bf16[1,128,256]{2,1,0:T(8,128)(2,1)S(1)} %get-tuple-element.55), channel_id=1, source_target_pairs={{0,1},{1,2},{2,3},{3,4},{4,5},{5,6},{6,7},{7,8},{8,9},{9,10},{10,1... | collective-permute-start | bytes 196616 | tf_op jit(solution)/shard_map/ppermute | solution.py:18
  10.5 10.2 %collective-permute-start.3 = (bf16[1,128,256]{2,1,0:T(8,128)(2,1)S(1)}, bf16[1,128,256]{2,1,0:T(8,128)(2,1)S(1)}, u32[]{:S(2)}, u32[]{:S(2)}) collective-permute-start(bf16[1,128,256]{2,1,0:T(8,128)(2,1)S(1)} %get-tuple-element.56), channel_id=1, source_target_pairs={{1,0},{2,1},{3,2},{4,3},{5,4},{6,5},{7,6},{8,7},{9,8},{10,9},{11,1... | collective-permute-start | bytes 196616 | tf_op jit(solution)/shard_map/ppermute | solution.py:20
  12.8 9.9 %copy-start.20 = (bf16[256,9,128]{2,0,1:T(8,128)(2,1)S(1)}, bf16[256,9,128]{2,0,1:T(8,128)(2,1)}, u32[]{:S(2)}) copy-start(bf16[256,9,128]{2,0,1:T(8,128)(2,1)} %param.14) | copy-start | bytes 1769476
  12.8 19.7 %collective-permute-start = (bf16[1,256,256]{2,1,0:T(8,128)(2,1)S(1)}, bf16[1,256,256]{2,1,0:T(8,128)(2,1)S(1)}, u32[]{:S(2)}, u32[]{:S(2)}) collective-permute-start(bf16[1,256,256]{2,1,0:T(8,128)(2,1)S(1)} %get-tuple-element.45), channel_id=1, source_target_pairs={{0,1},{1,2},{2,3},{3,4},{4,5},{5,6},{6,7},{7,8},{8,9},{9,10},{10,1... | collective-permute-start | bytes 393224 | tf_op jit(solution)/shard_map/ppermute | solution.py:18
  18.1 14.4 %collective-permute-start.1 = (bf16[1,256,256]{2,1,0:T(8,128)(2,1)S(1)}, bf16[1,256,256]{2,1,0:T(8,128)(2,1)S(1)}, u32[]{:S(2)}, u32[]{:S(2)}) collective-permute-start(bf16[1,256,256]{2,1,0:T(8,128)(2,1)S(1)} %get-tuple-element.46), channel_id=1, source_target_pairs={{1,0},{2,1},{3,2},{4,3},{5,4},{6,5},{7,6},{8,7},{9,8},{10,9},{11,1... | collective-permute-start | bytes 393224 | tf_op jit(solution)/shard_map/ppermute | solution.py:20
  27.2 5.9 %copy-start.1 = (bf16[1,8,256,256]{3,2,1,0:T(8,128)(2,1)S(1)}, bf16[1,8,256,256]{3,2,1,0:T(8,128)(2,1)}, u32[]{:S(2)}) copy-start(bf16[1,8,256,256]{3,2,1,0:T(8,128)(2,1)} %param.11) | copy-start | bytes 3145732
  34.2 2.4 copy-start.2
  35.7 2.8 copy-start.8
  38.4 37.7 %copy-start.25 = (f32[128]{0:T(128)S(1)}, f32[128]{0:T(128)}, u32[]{:S(2)}) copy-start(f32[128]{0:T(128)} %param.17) | copy-start | bytes 1540
  38.4 37.7 %copy-start.32 = (f32[128]{0:T(128)S(1)}, f32[128]{0:T(128)}, u32[]{:S(2)}) copy-start(f32[128]{0:T(128)} %param.18) | copy-start | bytes 1540
  40.0 36.7 %copy-start.34 = (f32[128]{0:T(128)S(1)}, f32[128]{0:T(128)}, u32[]{:S(2)}) copy-start(f32[128]{0:T(128)} %param.16) | copy-start | bytes 1540
  40.0 36.7 %copy-start.36 = (f32[128]{0:T(128)S(1)}, f32[128]{0:T(128)}, u32[]{:S(2)}) copy-start(f32[128]{0:T(128)} %param.15) | copy-start | bytes 1540
  76.3 2.5 copy-start.24
  76.3 40.2 %copy-start.23 = (f32[2048]{0:T(1024)S(1)}, f32[2048]{0:T(1024)}, u32[]{:S(2)}) copy-start(f32[2048]{0:T(1024)} %compare_convert_fusion) | copy-start | bytes 24580
  116.4 5.4 %copy-start.12 = (bf16[8,256,256]{2,1,0:T(8,128)(2,1)S(1)}, bf16[8,256,256]{2,1,0:T(8,128)(2,1)}, u32[]{:S(2)}) copy-start(bf16[8,256,256]{2,1,0:T(8,128)(2,1)} %copy-done.11) | copy-start | bytes 3145732
  121.8 4.3 %copy-start.33 = (f32[128]{0:T(128)S(1)}, f32[128]{0:T(128)}, u32[]{:S(2)}) copy-start(f32[128]{0:T(128)} %param.18) | copy-start | bytes 1540
  189.6 2.5 copy-start.5
  189.6 3.6 %copy-start.3 = (bf16[8,256,256]{2,1,0:T(8,128)(2,1)S(1)}, bf16[8,256,256]{2,1,0:T(8,128)(2,1)}, u32[]{:S(2)}) copy-start(bf16[8,256,256]{2,1,0:T(8,128)(2,1)} %copy-done.2) | copy-start | bytes 3145732
  196.5 2.4 copy-start.7
  197.8 2.4 copy-start.27
  200.1 5.4 %copy-start.17 = (f32[512,128]{1,0:T(8,128)S(1)}, f32[512,128]{1,0:T(8,128)}, u32[]{:S(2)}) copy-start(f32[512,128]{1,0:T(8,128)} %get-tuple-element.34) | copy-start | bytes 786436
  209.7 82.7 %all-reduce.7.cloned.1.call-start = ((), (), s32[]{:S(2)}) async-start(), calls=%async_computation.2 | async-start | bytes 294912 | tf_op jit(solution)/shard_map/psum | solution.py:195
  (21 other events, 35.6 us)
Sparse Core Ops, SparseCore 0:
  209.8 59.5 reduce-scatter.1
  271.6 20.6 all-reduce.6
